TPU v7x, 256 devices: a whole 4x4x8 slice. The times are simulated.
256 devices in a mesh: dp: 32 (over y, x, core), mp: 8 (over z).
Axes of the slice: x: 4, y: 4, z: 8, core: 2. Of those that a mesh axis runs over, the one named last changes fastest.
Arguments:
- hidden: bfloat16 [16384, 4096], P('dp', 'mp'), may hold values from -50 to 50
- norm_gain: float32 [4096], replicated, may hold values from 0.1 to 1.9
- w_query: bfloat16 [4096, 4096], P(None, 'mp'), may hold values from -0.09375 to 0.09375
- w_out: bfloat16 [4096, 4096], P('mp'), may hold values from -0.09375 to 0.09375
- nb_keys: bfloat16 [256, 128, 4096], P('dp', None, 'mp'), may hold values from -250 to 250
- nb_values: bfloat16 [256, 128, 4096], P('dp', None, 'mp'), may hold values from -10 to 10
- neighbours: int32 [256, 2], P('dp'), may hold values from 0 to 255, as said below
- valid_spans: int32 [32], P('dp'), may hold values from 6 to 8, as said below
Outputs:
- mixed: float32 [16384, 4096], P('dp', 'mp')
Inputs may be any that keep to these rules, and one draw needn't show every extreme that they name: Block ids; block b is stored by index b // 8 of dp, its owner. The two neighbours of a span have different owners. The spans of one index of dp name one owner at most 2 times, and some owner is named exactly 2 times by the live spans of every index of dp. `valid_spans`: some index of dp has all 8 spans live.
All inputs are finite; a program needn't handle non-finite values.
Results may differ from a plain program's by a relative error of at most 0.0066.
Values may be sent and summed in bfloat16 or wider, within the bound.
No kernel may reach another device: no remote copies, remote signals or barrier semaphores. Data moves between devices by JAX's collectives and lax.ppermute only.
A program may use at most 128 MiB of HBM per device.

v0:
```python
import math
import jax
import jax.numpy as jnp
from jax import lax
from jax.sharding import PartitionSpec as P

HS = 128
SPAN = 64
eps = 1e-05


def shifted(block, axis, distance):
    devices = range(lax.axis_size(axis))
    route = [(i - distance, i) for i in devices if i - distance in devices]
    return lax.ppermute(block, axis, route)


def partial_attention(query_rows, key_rows, value_rows):
    inner_width = key_rows.shape[-1]
    head_count = inner_width // HS
    query_heads = query_rows.reshape(query_rows.shape[:-1] + (head_count, HS))
    key_heads = key_rows.reshape(key_rows.shape[:-1] + (head_count, HS))
    value_heads = value_rows.reshape(value_rows.shape[:-1] + (head_count, HS))
    factor = 1.0 / math.sqrt(HS)
    scores = (
        jnp.einsum(
            "...qhd,...khd->...qhk", query_heads, key_heads, preferred_element_type=jnp.float32
        )
        * factor
    )
    score_top = jnp.max(scores, axis=-1)
    weights = jnp.exp(scores - score_top[..., None])
    weight_sum = jnp.sum(weights, axis=-1)
    summed = jnp.einsum(
        "...qhk,...khd->...qhd",
        weights.astype(jnp.bfloat16),
        value_heads,
        preferred_element_type=jnp.float32,
    )
    part_out = (summed / weight_sum[..., None]).astype(jnp.bfloat16)
    return (part_out.reshape(part_out.shape[:-2] + (inner_width,)), score_top, weight_sum)


def combine(part_out, score_top, weight_sum):
    head_count = score_top.shape[-1]
    best_score = jnp.max(score_top, axis=1, keepdims=True)
    mix_weight = jnp.exp(score_top - best_score) * weight_sum
    widened = part_out.reshape(part_out.shape[:-1] + (head_count, HS)).astype(jnp.float32)
    merged = (
        jnp.sum(widened * mix_weight[..., None], axis=1) / jnp.sum(mix_weight, axis=1)[..., None]
    )
    return merged.reshape(merged.shape[:-2] + (head_count * HS,)).astype(jnp.bfloat16)


def shards(hidden, norm_gain, w_query, w_out, nb_keys, nb_values, neighbours, valid_spans):
    tok_rows = hidden.shape[0]
    span_dev = tok_rows // SPAN
    stored = nb_keys.shape[0]
    inner_width = w_query.shape[1]
    peer_count = lax.axis_size("dp")
    most_slots = max(2, (2 * span_dev + peer_count - 1) // peer_count)
    widened = lax.all_gather(hidden, "mp", axis=1, tiled=True).astype(jnp.float32)
    normed = (
        widened * lax.rsqrt(jnp.mean(widened * widened, axis=1, keepdims=True) + eps) * norm_gain
    ).astype(jnp.bfloat16)
    queries = jnp.dot(normed, w_query, preferred_element_type=jnp.float32).astype(jnp.bfloat16)
    following = shifted(queries[: SPAN - 1], "dp", -1)
    grouped = jnp.concatenate([queries[SPAN - 1 :], following], axis=0).reshape(
        span_dev, SPAN, inner_width
    )
    live_span = jnp.arange(span_dev, dtype=jnp.int32) < valid_spans[0]
    owners = (neighbours // stored).reshape(-1)
    slot_ids = (neighbours % stored).reshape(-1)
    is_live = jnp.repeat(live_span, 2)
    req_order = jnp.arange(owners.shape[0], dtype=jnp.int32)
    earlier = (
        (owners[:, None] == owners[None, :])
        & is_live[None, :]
        & (req_order[None, :] < req_order[:, None])
    )
    slot_rank = jnp.minimum(jnp.sum(earlier.astype(jnp.int32), axis=1), most_slots - 1)
    target = jnp.where(is_live, owners * most_slots + slot_rank, -1)
    slot_match = target[:, None] == jnp.arange(peer_count * most_slots, dtype=jnp.int32)[None, :]
    filled = jnp.any(slot_match, axis=0)
    request_table = jnp.where(
        filled, jnp.sum(jnp.where(slot_match, slot_ids[:, None], 0), axis=0), -1
    )
    request_table = request_table.reshape(peer_count, most_slots)
    source_span = jnp.sum(jnp.where(slot_match, req_order[:, None] // 2, 0), axis=0)
    sent_rows = grouped[source_span].reshape(peer_count, most_slots, SPAN, inner_width)
    wanted = lax.all_to_all(request_table, "dp", split_axis=0, concat_axis=0, tiled=True)
    asked = lax.all_to_all(sent_rows, "dp", split_axis=0, concat_axis=0, tiled=True)
    safe_ids = jnp.maximum(wanted, 0)
    result = partial_attention(asked, nb_keys[safe_ids], nb_values[safe_ids])
    part_back = lax.all_to_all(
        result[0].astype(jnp.float32), "dp", split_axis=0, concat_axis=0, tiled=True
    ).astype(jnp.bfloat16)
    top_back = lax.all_to_all(result[1], "dp", split_axis=0, concat_axis=0, tiled=True)
    sum_back = lax.all_to_all(result[2], "dp", split_axis=0, concat_axis=0, tiled=True)
    part_out = part_back[owners, slot_rank].reshape(span_dev, 2, SPAN, inner_width)
    score_top = top_back[owners, slot_rank].reshape(span_dev, 2, SPAN, -1)
    weight_sum = sum_back[owners, slot_rank].reshape(span_dev, 2, SPAN, -1)
    merged = combine(part_out, score_top, weight_sum)
    merged = jnp.where(live_span[:, None, None], merged, jnp.zeros_like(merged))
    flat_rows = merged.reshape(tok_rows, inner_width)
    previous = shifted(flat_rows[tok_rows - SPAN + 1 :], "dp", 1)
    placed = jnp.concatenate([previous, flat_rows[: tok_rows - SPAN + 1]], axis=0)
    head_terms = jnp.dot(placed, w_out, preferred_element_type=jnp.float32)
    summed = lax.psum_scatter(head_terms, "mp", scatter_dimension=1, tiled=True)
    return hidden.astype(jnp.float32) + summed


def solution(mesh):
    placed = (
        P("dp", "mp"),
        P(),
        P(None, "mp"),
        P("mp", None),
        P("dp", None, "mp"),
        P("dp", None, "mp"),
        P("dp", None),
        P("dp"),
    )
    return jax.shard_map(
        shards, mesh=mesh, in_specs=placed, out_specs=P("dp", "mp"), check_vma=False
    )
```

profile of v0, /device:TPU:1, one launch (start us, length us, event | category | flops | bytes accessed | tf_op | source)
XLA Modules:
  0.0 369.9 jit_solution(1386096142998444938)
XLA Ops:
  10.2 8.6 %all-to-all-start = ((s32[32,1,2]{2,1,0:T(1,128)}), s32[32,1,2]{2,1,0:T(1,128)S(1)}, u32[]{:S(2)}, u32[]{:S(2)}) async-start(s32[32,1,2]{2,1,0:T(1,128)} %bitcast.1), calls=%async_computation | async-start | bytes 32768 | tf_op jit(solution)/shard_map/all_to_all | solution.py:91
  18.8 48.7 %all-gather.2.cloned.1.call-done = bf16[512,4096]{1,0:T(8,128)(2,1)} async-done(((bf16[512,512]{1,0:T(8,128)(2,1)}), bf16[512,4096]{1,0:T(8,128)(2,1)}) %all-gather.2.cloned.1.call-update) | async-done | bytes 4194320 | tf_op jit(solution)/shard_map/all_gather | solution.py:62
  67.5 3.1 fusion
  70.6 5.9 %fusion.24 = bf16[512,512]{1,0:T(8,128)(2,1)S(1)} fusion(bf16[4096,512]{1,0:T(8,128)(2,1)} %param.10, bf16[512,4096]{1,0:T(8,128)(2,1)} %all-gather.2.cloned.1.call-done, f32[4096]{0:T(1024)} %param.9, f32[512]{0:T(512)S(1)} %add_rsqrt_fusion), kind=kOutput, calls=%fused_computation.32 | convolution fusion | flops 2156134400 | bytes 8931328 | tf_op jit(solution)/shard_map/dot_general | solution.py:66
  76.5 2.8 collective-permute-start
  79.4 2.9 collective-permute-done
  82.3 2.8 gather_fusion.2
  85.1 8.7 %all-to-all-start.1 = ((bf16[32,2,64,512]{3,2,1,0:T(8,128)(2,1)}), bf16[32,2,64,512]{3,2,1,0:T(8,128)(2,1)}, u32[]{:S(2)}, u32[]{:S(2)}) async-start(bf16[32,2,64,512]{3,2,1,0:T(8,128)(2,1)} %bitcast.69), calls=%async_computation.1 | async-start | bytes 8388608 | tf_op jit(solution)/shard_map/all_to_all | solution.py:92
  93.9 5.3 %gather_fusion.1 = bf16[64,128,512]{2,1,0:T(8,128)(2,1)} fusion(bf16[8,128,512]{2,1,0:T(8,128)(2,1)S(1)} %copy-done, s32[1024]{0:T(1024)S(1)} %pad_clamp_fusion.1), kind=kCustom, calls=%fused_computation.1 | custom fusion | bytes 16777472 | tf_op jit(solution)/shard_map/gather | solution.py:94
  99.3 12.6 %reshape.223 = bf16[32,2,128,4,128]{4,3,2,1,0:T(4,128)(2,1)} reshape(bf16[64,128,512]{2,1,0:T(8,128)(2,1)} %gather_fusion.1) | data formatting | bytes 16777216 | tf_op jit(solution)/shard_map/reshape | solution.py:22
  111.9 5.3 %gather_fusion = bf16[64,128,512]{2,1,0:T(8,128)(2,1)} fusion(bf16[8,128,512]{2,1,0:T(8,128)(2,1)S(1)} %copy-done.2, s32[1024]{0:T(1024)S(1)} %pad_clamp_fusion.1), kind=kCustom, calls=%fused_computation | custom fusion | bytes 16777472 | tf_op jit(solution)/shard_map/gather | solution.py:94
  117.3 12.5 %reshape.222 = bf16[32,2,128,4,128]{4,3,2,1,0:T(4,128)(2,1)} reshape(bf16[64,128,512]{2,1,0:T(8,128)(2,1)} %gather_fusion) | data formatting | bytes 16777216 | tf_op jit(solution)/shard_map/reshape | solution.py:23
  129.8 14.7 %all-to-all-done.1 = bf16[32,2,64,512]{3,2,1,0:T(8,128)(2,1)} async-done(((bf16[32,2,64,512]{3,2,1,0:T(8,128)(2,1)}), bf16[32,2,64,512]{3,2,1,0:T(8,128)(2,1)}, u32[]{:S(2)}, u32[]{:S(2)}) %all-to-all-start.1) | async-done | bytes 4194336 | tf_op jit(solution)/shard_map/all_to_all | solution.py:92
  144.4 11.0 %bitcast_reduce_fusion = (f32[32,2,64,4]{2,3,1,0:T(4,128)S(1)}, f32[32,2,4,128,64]{3,4,2,1,0:T(8,128)}) fusion(bf16[32,2,128,4,128]{4,3,2,1,0:T(4,128)(2,1)} %reshape.223, bf16[32,2,64,512]{3,2,1,0:T(8,128)(2,1)} %all-to-all-done.1), kind=kOutput, calls=%fused_computation.15 | convolution fusion | flops 541048832 | bytes 21037056 | tf_op jit(solution)/shard_map/...qhd,...khd->...qhk/dot_general | solution.py:26
  156.2 7.1 %all-to-all-start.3 = ((f32[32,1,512]{2,1,0:T(1,128)}), f32[32,1,512]{2,1,0:T(1,128)S(1)}, u32[]{:S(2)}, u32[]{:S(2)}) async-start(f32[32,1,512]{2,1,0:T(1,128)} %reshape.289), calls=%async_computation.3 | async-start | bytes 131072 | tf_op jit(solution)/shard_map/all_to_all | solution.py:98
  163.3 6.9 %fusion.9 = f32[32,2,64,4]{2,3,1,0:T(4,128)S(1)} fusion(f32[32,2,4,128,64]{3,4,2,1,0:T(8,128)} %get-tuple-element.12, f32[32,2,64,4]{2,3,1,0:T(4,128)S(1)} %get-tuple-element.11), kind=kLoop, calls=%fused_computation.22 | loop fusion | flops 6275072 | bytes 8519680 | tf_op jit(solution)/shard_map/reduce_sum | solution.py:33
  171.0 7.5 %all-to-all-start.4 = ((f32[32,1,512]{2,1,0:T(1,128)}), f32[32,1,512]{2,1,0:T(1,128)S(1)}, u32[]{:S(2)}, u32[]{:S(2)}) async-start(f32[32,1,512]{2,1,0:T(1,128)} %reshape.287), calls=%async_computation.4 | async-start | bytes 131072 | tf_op jit(solution)/shard_map/all_to_all | solution.py:99
  178.5 9.0 %convert_bitcast_fusion = bf16[32,2,4,8,8,128]{5,4,3,2,1,0:T(8,128)(2,1)S(1)} fusion(f32[32,2,64,4]{2,3,1,0:T(4,128)S(1)} %fusion.9, bf16[32,2,128,4,128]{4,3,2,1,0:T(4,128)(2,1)} %reshape.222, f32[32,2,4,128,64]{3,4,2,1,0:T(8,128)} %get-tuple-element.12, f32[32,2,64,4]{2,3,1,0:T(4,128)S(1)} %get-tuple-element.11), kind=kOutput, calls=%fused_computation.21 | convolution fusion | flops 547356672 | bytes 21102592 | tf_op jit(solution)/shard_map/...qhk,...khd->...qhd/dot_general | solution.py:34
  190.2 7.4 %all-to-all-start.2 = ((bf16[32,2,64,512]{3,2,1,0:T(8,128)(2,1)}), bf16[32,2,64,512]{3,2,1,0:T(8,128)(2,1)}, u32[]{:S(2)}, u32[]{:S(2)}) async-start(bf16[32,2,64,512]{3,2,1,0:T(8,128)(2,1)} %bitcast.68), calls=%async_computation.2 | async-start | bytes 8388608 | tf_op jit(solution)/shard_map/all_to_all | solution.py:95
  202.8 45.5 %all-to-all-done.2 = bf16[32,2,64,512]{3,2,1,0:T(8,128)(2,1)} async-done(((bf16[32,2,64,512]{3,2,1,0:T(8,128)(2,1)}), bf16[32,2,64,512]{3,2,1,0:T(8,128)(2,1)}, u32[]{:S(2)}, u32[]{:S(2)}) %all-to-all-start.2) | async-done | bytes 4194336 | tf_op jit(solution)/shard_map/all_to_all | solution.py:95
  248.3 2.8 gather_fusion.3
  255.4 4.3 %collective-permute-start.1 = (bf16[63,512]{1,0:T(8,128)(2,1)S(1)}, bf16[63,512]{1,0:T(8,128)(2,1)S(1)}, u32[]{:S(2)}, u32[]{:S(2)}) collective-permute-start(bf16[63,512]{1,0:T(8,128)(2,1)S(1)} %slice.30), channel_id=1, source_target_pairs={{0,8},{8,16},{16,24},{24,32},{32,40},{40,48},{48,56},{56,64},{64,7... | collective-permute-start | bytes 193544 | tf_op jit(solution)/shard_map/ppermute | solution.py:15
  261.1 5.6 %fusion.27 = f32[512,4096]{1,0:T(8,128)} fusion(bf16[512,4096]{1,0:T(8,128)(2,1)S(1)} %copy-done.3, bf16[449,512]{1,0:T(8,128)(2,1)S(1)} %slice.31, bf16[63,512]{1,0:T(8,128)(2,1)S(1)} %collective-permute-done.1), kind=kOutput, calls=%fused_computation.37 | convolution fusion | flops 2148532224 | bytes 13107200 | tf_op jit(solution)/shard_map/dot_general | solution.py:108
  266.7 94.0 %reduce-scatter.2.cloned.1.call-done = f32[512,512]{1,0:T(8,128)} async-done(((f32[512,4096]{1,0:T(8,128)}), f32[512,512]{1,0:T(8,128)}) %reduce-scatter.2.cloned.1.call-update) | async-done | bytes 1048592 | tf_op jit(solution)/shard_map/reduce_scatter | solution.py:109
  (66 shorter events, 20.6 us)
Async XLA Ops:
  6.5 87.4 %copy-start = (bf16[8,128,512]{2,1,0:T(8,128)(2,1)S(1)}, bf16[8,128,512]{2,1,0:T(8,128)(2,1)}, u32[]{:S(2)}) copy-start(bf16[8,128,512]{2,1,0:T(8,128)(2,1)} %param.12) | copy-start | bytes 3145732
  6.5 61.0 %all-gather.2.cloned.1.call-start = ((), (), s32[]{:S(2)}) async-start(), calls=%async_computation.6 | async-start | bytes 4718592 | tf_op jit(solution)/shard_map/all_gather | solution.py:62
  10.2 74.9 %all-to-all-start = ((s32[32,1,2]{2,1,0:T(1,128)}), s32[32,1,2]{2,1,0:T(1,128)S(1)}, u32[]{:S(2)}, u32[]{:S(2)}) async-start(s32[32,1,2]{2,1,0:T(1,128)} %bitcast.1), calls=%async_computation | async-start | bytes 32768 | tf_op jit(solution)/shard_map/all_to_all | solution.py:91
  76.5 5.8 %collective-permute-start = (bf16[63,512]{1,0:T(8,128)(2,1)S(1)}, bf16[63,512]{1,0:T(8,128)(2,1)S(1)}, u32[]{:S(2)}, u32[]{:S(2)}) collective-permute-start(bf16[63,512]{1,0:T(8,128)(2,1)S(1)} %slice.29), channel_id=1, source_target_pairs={{8,0},{16,8},{24,16},{32,24},{40,32},{48,40},{56,48},{64,56},{72,6... | collective-permute-start | bytes 193544 | tf_op jit(solution)/shard_map/ppermute | solution.py:15
  85.1 59.4 %all-to-all-start.1 = ((bf16[32,2,64,512]{3,2,1,0:T(8,128)(2,1)}), bf16[32,2,64,512]{3,2,1,0:T(8,128)(2,1)}, u32[]{:S(2)}, u32[]{:S(2)}) async-start(bf16[32,2,64,512]{3,2,1,0:T(8,128)(2,1)} %bitcast.69), calls=%async_computation.1 | async-start | bytes 8388608 | tf_op jit(solution)/shard_map/all_to_all | solution.py:92
  99.3 12.6 %copy-start.2 = (bf16[8,128,512]{2,1,0:T(8,128)(2,1)S(1)}, bf16[8,128,512]{2,1,0:T(8,128)(2,1)}, u32[]{:S(2)}) copy-start(bf16[8,128,512]{2,1,0:T(8,128)(2,1)} %param.13) | copy-start | bytes 3145732
  156.2 14.8 %all-to-all-start.3 = ((f32[32,1,512]{2,1,0:T(1,128)}), f32[32,1,512]{2,1,0:T(1,128)S(1)}, u32[]{:S(2)}, u32[]{:S(2)}) async-start(f32[32,1,512]{2,1,0:T(1,128)} %reshape.289), calls=%async_computation.3 | async-start | bytes 131072 | tf_op jit(solution)/shard_map/all_to_all | solution.py:98
  171.0 19.2 %all-to-all-start.4 = ((f32[32,1,512]{2,1,0:T(1,128)}), f32[32,1,512]{2,1,0:T(1,128)S(1)}, u32[]{:S(2)}, u32[]{:S(2)}) async-start(f32[32,1,512]{2,1,0:T(1,128)} %reshape.287), calls=%async_computation.4 | async-start | bytes 131072 | tf_op jit(solution)/shard_map/all_to_all | solution.py:99
  190.2 58.1 %all-to-all-start.2 = ((bf16[32,2,64,512]{3,2,1,0:T(8,128)(2,1)}), bf16[32,2,64,512]{3,2,1,0:T(8,128)(2,1)}, u32[]{:S(2)}, u32[]{:S(2)}) async-start(bf16[32,2,64,512]{3,2,1,0:T(8,128)(2,1)} %bitcast.68), calls=%async_computation.2 | async-start | bytes 8388608 | tf_op jit(solution)/shard_map/all_to_all | solution.py:95
  197.7 163.0 %reduce-scatter.2.cloned.1.call-start = ((), (), s32[]{:S(2)}) async-start(), calls=%async_computation.7 | async-start | bytes 9437184 | tf_op jit(solution)/shard_map/reduce_scatter | solution.py:109
  251.9 9.2 %copy-start.3 = (bf16[512,4096]{1,0:T(8,128)(2,1)S(1)}, bf16[512,4096]{1,0:T(8,128)(2,1)}, u32[]{:S(2)}) copy-start(bf16[512,4096]{1,0:T(8,128)(2,1)} %param.11) | copy-start | bytes 12582916
  255.4 5.6 %collective-permute-start.1 = (bf16[63,512]{1,0:T(8,128)(2,1)S(1)}, bf16[63,512]{1,0:T(8,128)(2,1)S(1)}, u32[]{:S(2)}, u32[]{:S(2)}) collective-permute-start(bf16[63,512]{1,0:T(8,128)(2,1)S(1)} %slice.30), channel_id=1, source_target_pairs={{0,8},{8,16},{16,24},{24,32},{32,40},{40,48},{48,56},{56,64},{64,7... | collective-permute-start | bytes 193544 | tf_op jit(solution)/shard_map/ppermute | solution.py:15
  259.8 100.9 %copy-start.4 = (bf16[512,512]{1,0:T(8,128)(2,1)S(1)}, bf16[512,512]{1,0:T(8,128)(2,1)}, u32[]{:S(2)}) copy-start(bf16[512,512]{1,0:T(8,128)(2,1)} %param.8) | copy-start | bytes 1572868
  261.1 102.0 %copy-start.1 = (bf16[8,128,512]{2,1,0:T(8,128)(2,1)S(1)}, bf16[8,128,512]{2,1,0:T(8,128)(2,1)}, u32[]{:S(2)}) copy-start(bf16[8,128,512]{2,1,0:T(8,128)(2,1)} %param.12) | copy-start | bytes 3145732
Sparse Core Ops, SparseCore 0:
  9.1 58.3 all-gather.1
  266.8 93.8 reduce-scatter.1
where the time goes:
time: 371 us; the launch traced here: 370 us
  waiting for transfers between devices  208 us (56%)
  local copies, waits for them, and re-layouts  51.2 us (14%)
  starting transfers between devices  46.4 us (13%)
  matrix products  31.4 us (8%)
  other arithmetic  18.7 us (5%)
  between operations  14.3 us (4%)
    reduce_scatter x1, waiting for transfers between devices, shards(): summed = lax.psum_scatter(head_terms, 'mp', scatter_dimension=1, tiled=True)  94 us
    all_gather x1, waiting for transfers between devices, shards(): lax.all_gather(hidden, 'mp', axis=1, tiled=True).astype(jnp.float32)  48.7 us
    all_to_all x1, waiting for transfers between devices, shards(): lax.all_to_all(result[0].astype(jnp.float32), 'dp', split_axis=0, concat_...  45.5 us
    all_to_all x1, waiting for transfers between devices, shards(): lax.all_to_all(sent_rows, 'dp', split_axis=0, concat_axis=0, tiled=True)  14.7 us
    reshape x1, local copies, waits for them, and re-layouts, partial_attention(): key_heads = key_rows.reshape(key_rows.shape[:-1] + (head_count, HS))  12.6 us
    reshape x1, local copies, waits for them, and re-layouts, partial_attention(): value_heads = value_rows.reshape(value_rows.shape[:-1] + (head_count, HS))  12.5 us
    dot_general x1, matrix products, partial_attention(): jnp.einsum('...qhd,...khd->...qhk', query_heads, key_heads, preferred_ele...  11 us
    gather x2, local copies, waits for them, and re-layouts, shards(): result = partial_attention(asked, nb_keys[safe_ids], nb_values[safe_ids])  10.7 us
  transfers between devices with their start and end apart: 9, of which 6 were waited for; matrix products, arithmetic and copies ran while one was open for 20% of the time, Pallas kernels for 0%

commit v1 on v0

--- a/solution.py
+++ b/solution.py
@@ -7,6 +7,13 @@
 HS = 128
 SPAN = 64
 eps = 1e-05
+
+
+def exchange_gather(block, axis, dim):
+    size = lax.axis_size(axis)
+    blocks = jnp.stack([block for _ in range(size)])
+    blocks = lax.all_to_all(blocks, axis, split_axis=0, concat_axis=0)
+    return jnp.concatenate(blocks, axis=dim)
 
 
 def shifted(block, axis, distance):
@@ -59,7 +66,7 @@
     inner_width = w_query.shape[1]
     peer_count = lax.axis_size("dp")
     most_slots = max(2, (2 * span_dev + peer_count - 1) // peer_count)
-    widened = lax.all_gather(hidden, "mp", axis=1, tiled=True).astype(jnp.float32)
+    widened = exchange_gather(hidden, "mp", 1).astype(jnp.float32)
     normed = (
         widened * lax.rsqrt(jnp.mean(widened * widened, axis=1, keepdims=True) + eps) * norm_gain
     ).astype(jnp.bfloat16)

time: 371 us -> 424 us (1.14)
  waiting for transfers between devices: 208 us -> 251 us
  starting transfers between devices: 46.4 us -> 54.1 us
    all_to_all x0 -> x1, waiting for transfers between devices: none -> 94.6 us  [exchange_gather(): blocks = lax.all_to_all(blocks, axis, split_axis=0, concat_axis=0)]
    all_gather x1 -> x0, waiting for transfers between devices: 48.7 us -> none  [shards(): lax.all_gather(hidden, 'mp', axis=1, tiled=True).astype(jnp.float32)]
    all_to_all x0 -> x1, starting transfers between devices: none -> 9 us  [exchange_gather(): blocks = lax.all_to_all(blocks, axis, split_axis=0, concat_axis=0)]
  transfers between devices with their start and end apart: 9 -> 9, of which waited for: 6 -> 6; matrix products, arithmetic and copies ran while one was open for 20% -> 17% of each run, Pallas kernels for 0% -> 0%
where the time goes in v1:
time: 424 us; the launch traced here: 423 us
  waiting for transfers between devices  251 us (59%)
  local copies, waits for them, and re-layouts  54.9 us (13%)
  starting transfers between devices  54.1 us (13%)
  matrix products  28 us (7%)
  other arithmetic  21 us (5%)
  between operations  14.4 us (3%)
    all_to_all x1, waiting for transfers between devices, exchange_gather(): blocks = lax.all_to_all(blocks, axis, split_axis=0, concat_axis=0)  94.6 us
    reduce_scatter x1, waiting for transfers between devices, shards(): summed = lax.psum_scatter(head_terms, 'mp', scatter_dimension=1, tiled=True)  91.5 us
    all_to_all x1, waiting for transfers between devices, shards(): lax.all_to_all(result[0].astype(jnp.float32), 'dp', split_axis=0, concat_...  45.5 us
    all_to_all x1, waiting for transfers between devices, shards(): lax.all_to_all(sent_rows, 'dp', split_axis=0, concat_axis=0, tiled=True)  14.7 us
    reshape x1, local copies, waits for them, and re-layouts, partial_attention(): key_heads = key_rows.reshape(key_rows.shape[:-1] + (head_count, HS))  12.6 us
    reshape x1, local copies, waits for them, and re-layouts, partial_attention(): value_heads = value_rows.reshape(value_rows.shape[:-1] + (head_count, HS))  12.5 us
    dot_general x1, matrix products, partial_attention(): jnp.einsum('...qhd,...khd->...qhk', query_heads, key_heads, preferred_ele...  11 us
    gather x2, local copies, waits for them, and re-layouts, shards(): result = partial_attention(asked, nb_keys[safe_ids], nb_values[safe_ids])  10.7 us
  transfers between devices with their start and end apart: 9, of which 6 were waited for; matrix products, arithmetic and copies ran while one was open for 17% of the time, Pallas kernels for 0%

profile of v1, /device:TPU:1, one launch (start us, length us, event | category | flops | bytes accessed | tf_op | source)
XLA Modules:
  0.0 423.2 jit_solution(6970384313722825568)
XLA Ops:
  10.2 9.0 %all-to-all-start.1 = ((bf16[8,512,512]{1,2,0:T(8,128)(2,1)}), bf16[8,512,512]{1,2,0:T(8,128)(2,1)}, u32[]{:S(2)}, u32[]{:S(2)}) async-start(bf16[8,512,512]{1,2,0:T(8,128)(2,1)} %stack.2), calls=%async_computation.1 | async-start | bytes 8388608 | tf_op jit(solution)/shard_map/all_to_all | solution.py:15
  21.5 94.6 %all-to-all-done.1 = bf16[8,512,512]{1,2,0:T(8,128)(2,1)} async-done(((bf16[8,512,512]{1,2,0:T(8,128)(2,1)}), bf16[8,512,512]{1,2,0:T(8,128)(2,1)}, u32[]{:S(2)}, u32[]{:S(2)}) %all-to-all-start.1) | async-done | bytes 4194336 | tf_op jit(solution)/shard_map/all_to_all | solution.py:15
  116.1 7.6 %all-to-all-start = ((s32[32,1,2]{2,1,0:T(1,128)}), s32[32,1,2]{2,1,0:T(1,128)S(1)}, u32[]{:S(2)}, u32[]{:S(2)}) async-start(s32[32,1,2]{2,1,0:T(1,128)} %bitcast.1), calls=%async_computation | async-start | bytes 32768 | tf_op jit(solution)/shard_map/all_to_all | solution.py:98
  123.7 3.3 multiply_reduce_fusion
  127.0 2.8 fusion.1
  134.5 3.3 collective-permute-done
  137.8 2.8 gather_fusion.2
  140.6 9.0 %all-to-all-start.2 = ((bf16[32,2,64,512]{3,2,1,0:T(8,128)(2,1)}), bf16[32,2,64,512]{3,2,1,0:T(8,128)(2,1)}, u32[]{:S(2)}, u32[]{:S(2)}) async-start(bf16[32,2,64,512]{3,2,1,0:T(8,128)(2,1)} %bitcast.78), calls=%async_computation.2 | async-start | bytes 8388608 | tf_op jit(solution)/shard_map/all_to_all | solution.py:99
  149.8 5.3 %gather_fusion.1 = bf16[64,128,512]{2,1,0:T(8,128)(2,1)} fusion(bf16[8,128,512]{2,1,0:T(8,128)(2,1)S(1)} %copy-done, s32[1024]{0:T(1024)S(1)} %pad_clamp_fusion.1), kind=kCustom, calls=%fused_computation.1 | custom fusion | bytes 16777472 | tf_op jit(solution)/shard_map/gather | solution.py:101
  155.1 12.6 %reshape.229 = bf16[32,2,128,4,128]{4,3,2,1,0:T(4,128)(2,1)} reshape(bf16[64,128,512]{2,1,0:T(8,128)(2,1)} %gather_fusion.1) | data formatting | bytes 16777216 | tf_op jit(solution)/shard_map/reshape | solution.py:29
  167.7 5.3 %gather_fusion = bf16[64,128,512]{2,1,0:T(8,128)(2,1)} fusion(bf16[8,128,512]{2,1,0:T(8,128)(2,1)S(1)} %copy-done.2, s32[1024]{0:T(1024)S(1)} %pad_clamp_fusion.1), kind=kCustom, calls=%fused_computation | custom fusion | bytes 16777472 | tf_op jit(solution)/shard_map/gather | solution.py:101
  173.1 12.5 %reshape.228 = bf16[32,2,128,4,128]{4,3,2,1,0:T(4,128)(2,1)} reshape(bf16[64,128,512]{2,1,0:T(8,128)(2,1)} %gather_fusion) | data formatting | bytes 16777216 | tf_op jit(solution)/shard_map/reshape | solution.py:30
  185.6 14.7 %all-to-all-done.2 = bf16[32,2,64,512]{3,2,1,0:T(8,128)(2,1)} async-done(((bf16[32,2,64,512]{3,2,1,0:T(8,128)(2,1)}), bf16[32,2,64,512]{3,2,1,0:T(8,128)(2,1)}, u32[]{:S(2)}, u32[]{:S(2)}) %all-to-all-start.2) | async-done | bytes 4194336 | tf_op jit(solution)/shard_map/all_to_all | solution.py:99
  200.3 11.0 %bitcast_reduce_fusion = (f32[32,2,64,4]{2,3,1,0:T(4,128)S(1)}, f32[32,2,4,128,64]{3,4,2,1,0:T(8,128)}) fusion(bf16[32,2,128,4,128]{4,3,2,1,0:T(4,128)(2,1)} %reshape.229, bf16[32,2,64,512]{3,2,1,0:T(8,128)(2,1)} %all-to-all-done.2), kind=kOutput, calls=%fused_computation.13 | convolution fusion | flops 541048832 | bytes 21037056 | tf_op jit(solution)/shard_map/...qhd,...khd->...qhk/dot_general | solution.py:33
  212.1 7.1 %all-to-all-start.4 = ((f32[32,1,512]{2,1,0:T(1,128)}), f32[32,1,512]{2,1,0:T(1,128)S(1)}, u32[]{:S(2)}, u32[]{:S(2)}) async-start(f32[32,1,512]{2,1,0:T(1,128)} %reshape.296), calls=%async_computation.4 | async-start | bytes 131072 | tf_op jit(solution)/shard_map/all_to_all | solution.py:105
  219.2 6.9 %fusion.8 = f32[32,2,64,4]{2,3,1,0:T(4,128)S(1)} fusion(f32[32,2,4,128,64]{3,4,2,1,0:T(8,128)} %get-tuple-element.12, f32[32,2,64,4]{2,3,1,0:T(4,128)S(1)} %get-tuple-element.11), kind=kLoop, calls=%fused_computation.21 | loop fusion | flops 6275072 | bytes 8519680 | tf_op jit(solution)/shard_map/reduce_sum | solution.py:40
  226.8 7.5 %all-to-all-start.5 = ((f32[32,1,512]{2,1,0:T(1,128)}), f32[32,1,512]{2,1,0:T(1,128)S(1)}, u32[]{:S(2)}, u32[]{:S(2)}) async-start(f32[32,1,512]{2,1,0:T(1,128)} %reshape.294), calls=%async_computation.5 | async-start | bytes 131072 | tf_op jit(solution)/shard_map/all_to_all | solution.py:106
  234.3 9.0 %convert_bitcast_fusion = bf16[32,2,4,8,8,128]{5,4,3,2,1,0:T(8,128)(2,1)S(1)} fusion(f32[32,2,64,4]{2,3,1,0:T(4,128)S(1)} %fusion.8, bf16[32,2,128,4,128]{4,3,2,1,0:T(4,128)(2,1)} %reshape.228, f32[32,2,4,128,64]{3,4,2,1,0:T(8,128)} %get-tuple-element.12, f32[32,2,64,4]{2,3,1,0:T(4,128)S(1)} %get-tuple-element.11), kind=kOutput, calls=%fused_computation.19 | convolution fusion | flops 547356672 | bytes 21102592 | tf_op jit(solution)/shard_map/...qhk,...khd->...qhd/dot_general | solution.py:41
  246.1 7.4 %all-to-all-start.3 = ((bf16[32,2,64,512]{3,2,1,0:T(8,128)(2,1)}), bf16[32,2,64,512]{3,2,1,0:T(8,128)(2,1)}, u32[]{:S(2)}, u32[]{:S(2)}) async-start(bf16[32,2,64,512]{3,2,1,0:T(8,128)(2,1)} %bitcast.77), calls=%async_computation.3 | async-start | bytes 8388608 | tf_op jit(solution)/shard_map/all_to_all | solution.py:102
  258.7 45.5 %all-to-all-done.3 = bf16[32,2,64,512]{3,2,1,0:T(8,128)(2,1)} async-done(((bf16[32,2,64,512]{3,2,1,0:T(8,128)(2,1)}), bf16[32,2,64,512]{3,2,1,0:T(8,128)(2,1)}, u32[]{:S(2)}, u32[]{:S(2)}) %all-to-all-start.3) | async-done | bytes 4194336 | tf_op jit(solution)/shard_map/all_to_all | solution.py:102
  304.2 2.8 gather_fusion.3
  311.3 4.3 %collective-permute-start.1 = (bf16[63,512]{1,0:T(8,128)(2,1)S(1)}, bf16[63,512]{1,0:T(8,128)(2,1)S(1)}, u32[]{:S(2)}, u32[]{:S(2)}) collective-permute-start(bf16[63,512]{1,0:T(8,128)(2,1)S(1)} %slice.30), channel_id=1, source_target_pairs={{0,8},{8,16},{16,24},{24,32},{32,40},{40,48},{48,56},{56,64},{64,7... | collective-permute-start | bytes 193544 | tf_op jit(solution)/shard_map/ppermute | solution.py:22
  316.9 5.6 %fusion.19 = f32[512,4096]{1,0:T(8,128)} fusion(bf16[512,4096]{1,0:T(8,128)(2,1)S(1)} %copy-done.3, bf16[449,512]{1,0:T(8,128)(2,1)S(1)} %slice.31, bf16[63,512]{1,0:T(8,128)(2,1)S(1)} %collective-permute-done.1), kind=kOutput, calls=%fused_computation.33 | convolution fusion | flops 2148532224 | bytes 13107200 | tf_op jit(solution)/shard_map/dot_general | solution.py:115
  322.5 91.5 %reduce-scatter.2.cloned.1.call-done = f32[512,512]{1,0:T(8,128)} async-done(((f32[512,4096]{1,0:T(8,128)}), f32[512,512]{1,0:T(8,128)}) %reduce-scatter.2.cloned.1.call-update) | async-done | bytes 1048592 | tf_op jit(solution)/shard_map/reduce_scatter | solution.py:116
  (74 shorter events, 27.4 us)
Async XLA Ops:
  6.5 143.2 %copy-start = (bf16[8,128,512]{2,1,0:T(8,128)(2,1)S(1)}, bf16[8,128,512]{2,1,0:T(8,128)(2,1)}, u32[]{:S(2)}) copy-start(bf16[8,128,512]{2,1,0:T(8,128)(2,1)} %param.12) | copy-start | bytes 3145732
  6.5 13.5 %copy-start.6 = (s32[8,2]{0,1:T(2,128)S(1)}, s32[8,2]{0,1:T(2,128)}, u32[]{:S(2)}) copy-start(s32[8,2]{0,1:T(2,128)} %param.14) | copy-start | bytes 196
  7.9 119.1 %copy-start.5 = (f32[4096]{0:T(1024)S(1)}, f32[4096]{0:T(1024)}, u32[]{:S(2)}) copy-start(f32[4096]{0:T(1024)} %param.9) | copy-start | bytes 49156
  10.2 105.9 %all-to-all-start.1 = ((bf16[8,512,512]{1,2,0:T(8,128)(2,1)}), bf16[8,512,512]{1,2,0:T(8,128)(2,1)}, u32[]{:S(2)}, u32[]{:S(2)}) async-start(bf16[8,512,512]{1,2,0:T(8,128)(2,1)} %stack.2), calls=%async_computation.1 | async-start | bytes 8388608 | tf_op jit(solution)/shard_map/all_to_all | solution.py:15
  116.1 24.5 %all-to-all-start = ((s32[32,1,2]{2,1,0:T(1,128)}), s32[32,1,2]{2,1,0:T(1,128)S(1)}, u32[]{:S(2)}, u32[]{:S(2)}) async-start(s32[32,1,2]{2,1,0:T(1,128)} %bitcast.1), calls=%async_computation | async-start | bytes 32768 | tf_op jit(solution)/shard_map/all_to_all | solution.py:98
  123.7 6.1 %copy-start.7 = (bf16[4096,512]{1,0:T(8,128)(2,1)S(1)}, bf16[4096,512]{1,0:T(8,128)(2,1)}, u32[]{:S(2)}) copy-start(bf16[4096,512]{1,0:T(8,128)(2,1)} %param.10) | copy-start | bytes 12582916
  132.2 5.6 %collective-permute-start = (bf16[63,512]{1,0:T(8,128)(2,1)S(1)}, bf16[63,512]{1,0:T(8,128)(2,1)S(1)}, u32[]{:S(2)}, u32[]{:S(2)}) collective-permute-start(bf16[63,512]{1,0:T(8,128)(2,1)S(1)} %slice.29), channel_id=1, source_target_pairs={{8,0},{16,8},{24,16},{32,24},{40,32},{48,40},{56,48},{64,56},{72,6... | collective-permute-start | bytes 193544 | tf_op jit(solution)/shard_map/ppermute | solution.py:22
  140.6 59.7 %all-to-all-start.2 = ((bf16[32,2,64,512]{3,2,1,0:T(8,128)(2,1)}), bf16[32,2,64,512]{3,2,1,0:T(8,128)(2,1)}, u32[]{:S(2)}, u32[]{:S(2)}) async-start(bf16[32,2,64,512]{3,2,1,0:T(8,128)(2,1)} %bitcast.78), calls=%async_computation.2 | async-start | bytes 8388608 | tf_op jit(solution)/shard_map/all_to_all | solution.py:99
  155.1 12.6 %copy-start.2 = (bf16[8,128,512]{2,1,0:T(8,128)(2,1)S(1)}, bf16[8,128,512]{2,1,0:T(8,128)(2,1)}, u32[]{:S(2)}) copy-start(bf16[8,128,512]{2,1,0:T(8,128)(2,1)} %param.13) | copy-start | bytes 3145732
  212.1 14.8 %all-to-all-start.4 = ((f32[32,1,512]{2,1,0:T(1,128)}), f32[32,1,512]{2,1,0:T(1,128)S(1)}, u32[]{:S(2)}, u32[]{:S(2)}) async-start(f32[32,1,512]{2,1,0:T(1,128)} %reshape.296), calls=%async_computation.4 | async-start | bytes 131072 | tf_op jit(solution)/shard_map/all_to_all | solution.py:105
  226.8 19.2 %all-to-all-start.5 = ((f32[32,1,512]{2,1,0:T(1,128)}), f32[32,1,512]{2,1,0:T(1,128)S(1)}, u32[]{:S(2)}, u32[]{:S(2)}) async-start(f32[32,1,512]{2,1,0:T(1,128)} %reshape.294), calls=%async_computation.5 | async-start | bytes 131072 | tf_op jit(solution)/shard_map/all_to_all | solution.py:106
  246.1 58.1 %all-to-all-start.3 = ((bf16[32,2,64,512]{3,2,1,0:T(8,128)(2,1)}), bf16[32,2,64,512]{3,2,1,0:T(8,128)(2,1)}, u32[]{:S(2)}, u32[]{:S(2)}) async-start(bf16[32,2,64,512]{3,2,1,0:T(8,128)(2,1)} %bitcast.77), calls=%async_computation.3 | async-start | bytes 8388608 | tf_op jit(solution)/shard_map/all_to_all | solution.py:102
  253.5 160.5 %reduce-scatter.2.cloned.1.call-start = ((), (), s32[]{:S(2)}) async-start(), calls=%async_computation.7 | async-start | bytes 9437184 | tf_op jit(solution)/shard_map/reduce_scatter | solution.py:116
  307.7 9.2 %copy-start.3 = (bf16[512,4096]{1,0:T(8,128)(2,1)S(1)}, bf16[512,4096]{1,0:T(8,128)(2,1)}, u32[]{:S(2)}) copy-start(bf16[512,4096]{1,0:T(8,128)(2,1)} %param.11) | copy-start | bytes 12582916
  311.3 5.6 %collective-permute-start.1 = (bf16[63,512]{1,0:T(8,128)(2,1)S(1)}, bf16[63,512]{1,0:T(8,128)(2,1)S(1)}, u32[]{:S(2)}, u32[]{:S(2)}) collective-permute-start(bf16[63,512]{1,0:T(8,128)(2,1)S(1)} %slice.30), channel_id=1, source_target_pairs={{0,8},{8,16},{16,24},{24,32},{32,40},{40,48},{48,56},{56,64},{64,7... | collective-permute-start | bytes 193544 | tf_op jit(solution)/shard_map/ppermute | solution.py:22
  315.6 98.4 %copy-start.4 = (bf16[512,512]{1,0:T(8,128)(2,1)S(1)}, bf16[512,512]{1,0:T(8,128)(2,1)}, u32[]{:S(2)}) copy-start(bf16[512,512]{1,0:T(8,128)(2,1)} %param.8) | copy-start | bytes 1572868
  316.9 99.5 %copy-start.1 = (bf16[8,128,512]{2,1,0:T(8,128)(2,1)S(1)}, bf16[8,128,512]{2,1,0:T(8,128)(2,1)}, u32[]{:S(2)}) copy-start(bf16[8,128,512]{2,1,0:T(8,128)(2,1)} %param.12) | copy-start | bytes 3145732
Sparse Core Ops, SparseCore 0:
  322.6 91.3 reduce-scatter.1
